TPU v7x, 32 devices: a whole 2x2x4 slice. The times are simulated.
32 devices in a mesh: grp: 2 (over core), tp: 8 (over z, y), dp: 2 (over x).
Axes of the slice: x: 2, y: 2, z: 4, core: 2. Of those that a mesh axis runs over, the one named last changes fastest.
Arguments:
- base_inputs: bfloat16 [3, 128, 8192], P(None, 'dp', ('grp', 'tp')), may hold values from -6 to 6
- small_inputs: bfloat16 [2, 3, 128, 4096], P('grp', None, 'dp', 'tp'), may hold values from -6 to 6
- base_norm_gain: float32 [8192], replicated, may hold values from 0.1 to 1.9
- base_query: bfloat16 [8192, 8192], P(None, ('grp', 'tp')), may hold values from -0.0625 to 0.0625
- base_keys_values: bfloat16 [2, 8192, 1024], P(None, None, ('grp', 'tp')), may hold values from -0.0625 to 0.0625
- base_output: bfloat16 [8192, 8192], P(('grp', 'tp')), may hold values from -0.0625 to 0.0625
- base_cache: bfloat16 [2, 128, 1024, 128], P(None, 'dp', ('grp', 'tp')), may hold values from -600 to 600
- base_final_gain: float32 [8192], replicated, may hold values from 0.1 to 1.9
- base_unembed: bfloat16 [16384, 8192], P(('grp', 'tp')), may hold values from -20 to 20
- small_norm_gain: float32 [2, 4096], P('grp'), may hold values from 0.1 to 1.9
- small_projections: bfloat16 [2, 3, 4096, 4096], P('grp', None, None, 'tp'), may hold values from -0.09375 to 0.09375
- small_output: bfloat16 [2, 4096, 4096], P('grp', 'tp'), may hold values from -0.09375 to 0.09375
- small_cache: bfloat16 [2, 2, 128, 4096, 128], P('grp', None, 'dp', 'tp'), may hold values from -600 to 600
- small_final_gain: float32 [2, 4096], P('grp'), may hold values from 0.1 to 1.9
- small_unembed: bfloat16 [2, 2, 8192, 4096], P('grp', None, 'tp'), may hold values from -0.1875 to 0.1875
- lengths: int32 [128], P('dp'), may hold values from 1 to 128, as said below
- next_tokens: int32 [3, 128], P(None, 'dp'), may hold values from 0 to 16383
Outputs:
- log_probs: float32 [3, 128, 16384], P(None, 'dp', ('grp', 'tp'))
- chosen_total: float32 [128], P('dp')
Inputs may be any that keep to these rules, and one draw needn't show every extreme that they name: `lengths`: some row holds 128 cached positions.
All inputs are finite; a program needn't handle non-finite values.
Results may differ from a plain program's by a relative error of at most 0.0035.
Values may be sent and summed in bfloat16 or wider, within the bound.
A program may use at most 256 MiB of HBM per device.

v0:
```python
import math
import jax
import jax.numpy as jnp
from jax import lax
from jax.sharding import PartitionSpec as P

HD = 128
STEPS = 3
CACHE = 128
EPSILON = 1e-05
NEGATIVE = -1e30


def partner(array, axis, bit):
    return lax.ppermute(array, axis, [(i, i ^ 1 << bit) for i in range(lax.axis_size(axis))])


def rotate_pairs(values, positions, first_pair, head_size):
    pair_count = values.shape[-1] // 2
    pair_index = (first_pair + jnp.arange(pair_count)).astype(jnp.float32)
    frequency = jnp.exp(pair_index * (-2.0 * math.log(10000.0) / head_size))
    angles = positions.astype(jnp.float32)[:, None] * frequency[None, :]
    angles = angles.reshape((values.shape[0],) + (1,) * (values.ndim - 2) + (pair_count,))
    cosine = jnp.cos(angles)
    sine_part = jnp.sin(angles)
    paired = values.reshape(values.shape[:-1] + (pair_count, 2))
    even_part = paired[..., 0]
    odd_part = paired[..., 1]
    turned = jnp.stack(
        [even_part * cosine - odd_part * sine_part, even_part * sine_part + odd_part * cosine],
        axis=-1,
    )
    return turned.reshape(values.shape)


def norm_rows(values, gain_row):
    values = values.astype(jnp.float32)
    scaling = lax.rsqrt(jnp.mean(values * values, axis=-1, keepdims=True) + EPSILON)
    return (values * scaling * gain_row).astype(jnp.bfloat16)


def attention_weights(cached_scores, fresh_scores, visible, head_size):
    factor = 1.0 / math.sqrt(head_size)
    cached_scores = jnp.where(visible, cached_scores * factor, NEGATIVE)
    fresh_scores = fresh_scores * factor
    row_max = jnp.maximum(
        jnp.max(cached_scores, axis=-1, keepdims=True),
        jnp.max(fresh_scores, axis=-1, keepdims=True),
    )
    cached_exp = jnp.exp(cached_scores - row_max)
    fresh_exp = jnp.exp(fresh_scores - row_max)
    totals = jnp.sum(cached_exp, axis=-1, keepdims=True) + jnp.sum(
        fresh_exp, axis=-1, keepdims=True
    )
    return ((cached_exp / totals).astype(jnp.bfloat16), (fresh_exp / totals).astype(jnp.bfloat16))


def sum_slices(scores, share_count):
    for bit_index in range(share_count.bit_length() - 1):
        scores = scores + partner(scores, "tp", bit_index)
    return scores


def body(
    base_inputs,
    small_inputs,
    base_norm_gain,
    base_query,
    base_keys_values,
    base_output,
    base_cache,
    base_final_gain,
    base_unembed,
    small_norm_gain,
    small_projections,
    small_output,
    small_cache,
    small_final_gain,
    small_unembed,
    lengths,
    next_tokens,
):
    row_count = lengths.shape[0]
    slice_width = base_keys_values.shape[2]
    share_count = HD // slice_width
    group_size = base_query.shape[1] // slice_width
    slice_index = lax.axis_index("tp") % share_count
    first_pair = slice_index * (slice_width // 2)
    block_index = lax.axis_index(("grp", "tp"))
    vocab_width = base_unembed.shape[0]
    small_heads = small_projections.shape[3] // HD
    base_full = lax.all_gather(base_inputs, ("grp", "tp"), axis=2, tiled=True)
    small_full = lax.all_gather(small_inputs[0], "tp", axis=2, tiled=True)
    visible = (jnp.arange(CACHE)[None, :] < lengths[:, None])[:, None, :]
    base_keys_cache = base_cache[0]
    base_values_cache = base_cache[1]
    small_keys_cache = small_cache[0, 0].reshape(row_count, small_heads, HD, CACHE)
    small_values_cache = small_cache[0, 1].reshape(row_count, small_heads, HD, CACHE)
    small_table = small_unembed[0].reshape(-1, small_unembed.shape[3])
    base_new_keys = []
    base_new_values = []
    small_new_keys = []
    small_new_values = []
    log_steps = []
    chosen_total = jnp.zeros((row_count,), jnp.float32)
    for step_index in range(STEPS):
        positions = lengths + step_index
        small_normed = norm_rows(small_full[step_index], small_norm_gain[0])
        small_queries = jnp.dot(
            small_normed, small_projections[0, 0], preferred_element_type=jnp.float32
        ).reshape(row_count, small_heads, HD)
        small_queries = rotate_pairs(small_queries, positions, 0, HD).astype(jnp.bfloat16)
        small_key = jnp.dot(
            small_normed, small_projections[0, 1], preferred_element_type=jnp.float32
        ).reshape(row_count, small_heads, HD)
        small_new_keys.append(rotate_pairs(small_key, positions, 0, HD).astype(jnp.bfloat16))
        small_value = jnp.dot(
            small_normed, small_projections[0, 2], preferred_element_type=jnp.float32
        ).reshape(row_count, small_heads, HD)
        small_new_values.append(small_value.astype(jnp.bfloat16))
        small_fresh_keys = jnp.stack(small_new_keys, axis=-1)
        small_fresh_values = jnp.stack(small_new_values, axis=-1)
        small_cached_scores = jnp.einsum(
            "rhd,rhdl->rhl", small_queries, small_keys_cache, preferred_element_type=jnp.float32
        )
        small_fresh_scores = jnp.einsum(
            "rhd,rhdn->rhn", small_queries, small_fresh_keys, preferred_element_type=jnp.float32
        )
        small_cached_weights, small_fresh_weights = attention_weights(
            small_cached_scores, small_fresh_scores, visible, HD
        )
        small_head_values = jnp.einsum(
            "rhl,rhdl->rhd",
            small_cached_weights,
            small_values_cache,
            preferred_element_type=jnp.float32,
        )
        small_head_values = small_head_values + jnp.einsum(
            "rhn,rhdn->rhd",
            small_fresh_weights,
            small_fresh_values,
            preferred_element_type=jnp.float32,
        )
        small_head_values = small_head_values.astype(jnp.bfloat16).reshape(
            row_count, small_heads * HD
        )
        small_partial = jnp.dot(
            small_head_values, small_output[0], preferred_element_type=jnp.float32
        )
        small_mixed = lax.psum(small_partial, "tp")
        small_hidden = small_full[step_index].astype(jnp.float32) + small_mixed
        small_final = norm_rows(small_hidden, small_final_gain[0])
        small_logits = lax.dot_general(
            small_final, small_table, (((1,), (1,)), ((), ())), preferred_element_type=jnp.float32
        )
        small_logits = small_logits.reshape(row_count, 2, small_table.shape[0] // 2)
        paired_logits = lax.all_to_all(
            small_logits[None], "grp", split_axis=2, concat_axis=0, tiled=True
        )
        normed = norm_rows(base_full[step_index], base_norm_gain)
        queries = jnp.dot(normed, base_query, preferred_element_type=jnp.float32).reshape(
            row_count, group_size, slice_width
        )
        queries = rotate_pairs(queries, positions, first_pair, HD).astype(jnp.bfloat16)
        new_key = jnp.dot(normed, base_keys_values[0], preferred_element_type=jnp.float32)
        key_now = rotate_pairs(new_key, positions, first_pair, HD).astype(jnp.bfloat16)
        value_now = jnp.dot(normed, base_keys_values[1], preferred_element_type=jnp.float32).astype(
            jnp.bfloat16
        )
        base_new_keys.append(key_now)
        base_new_values.append(value_now)
        fresh_keys = jnp.stack(base_new_keys, axis=-1)
        fresh_values = jnp.stack(base_new_values, axis=-1)
        cached_scores = jnp.einsum(
            "rgd,rdl->rgl", queries, base_keys_cache, preferred_element_type=jnp.float32
        )
        fresh_scores = jnp.einsum(
            "rgd,rdn->rgn", queries, fresh_keys, preferred_element_type=jnp.float32
        )
        both_scores = sum_slices(
            jnp.concatenate([cached_scores, fresh_scores], axis=-1), share_count
        )
        cached_weights, fresh_weights = attention_weights(
            both_scores[..., :CACHE], both_scores[..., CACHE:], visible, HD
        )
        head_values = jnp.einsum(
            "rgl,rdl->rgd", cached_weights, base_values_cache, preferred_element_type=jnp.float32
        )
        head_values = head_values + jnp.einsum(
            "rgn,rdn->rgd", fresh_weights, fresh_values, preferred_element_type=jnp.float32
        )
        head_values = head_values.astype(jnp.bfloat16).reshape(row_count, group_size * slice_width)
        partial_value = jnp.dot(head_values, base_output, preferred_element_type=jnp.float32)
        mixed_sum = lax.psum(partial_value, ("grp", "tp"))
        hidden = base_full[step_index].astype(jnp.float32) + mixed_sum
        final_rows = norm_rows(hidden, base_final_gain)
        base_logits = lax.dot_general(
            final_rows, base_unembed, (((1,), (1,)), ((), ())), preferred_element_type=jnp.float32
        )
        steered = base_logits + paired_logits[0, :, 0] - paired_logits[1, :, 0]
        local_max = jnp.max(steered, axis=-1)
        token_local = next_tokens[step_index] - block_index * vocab_width
        token_hit = jnp.arange(vocab_width)[None, :] == token_local[:, None]
        picked_local = jnp.sum(jnp.where(token_hit, steered, 0.0), axis=-1)
        row_max = lax.pmax(local_max, ("grp", "tp"))
        exp_total, picked = lax.psum(
            (jnp.sum(jnp.exp(steered - row_max[:, None]), axis=-1), picked_local), ("grp", "tp")
        )
        log_norm = row_max + jnp.log(exp_total)
        log_steps.append(steered - log_norm[:, None])
        chosen_total = chosen_total + picked - log_norm
    return (jnp.stack(log_steps, axis=0), chosen_total)


def solution(mesh):
    placed = (
        P(None, "dp", ("grp", "tp")),
        P("grp", None, "dp", "tp"),
        P(),
        P(None, ("grp", "tp")),
        P(None, None, ("grp", "tp")),
        P(("grp", "tp"), None),
        P(None, "dp", ("grp", "tp"), None),
        P(),
        P(("grp", "tp"), None),
        P("grp", None),
        P("grp", None, None, "tp"),
        P("grp", "tp", None),
        P("grp", None, "dp", "tp", None),
        P("grp", None),
        P("grp", None, "tp", None),
        P("dp"),
        P(None, "dp"),
    )
    return jax.shard_map(
        body,
        mesh=mesh,
        in_specs=placed,
        out_specs=(P(None, "dp", ("grp", "tp")), P("dp")),
        check_vma=False,
    )
```

profile of v0, /device:TPU:0, one launch (start us, length us, event | category | flops | bytes accessed | tf_op | source)
XLA Modules:
  0.0 661.0 jit_solution(7503122877806506709)
XLA Ops:
  8.8 9.1 %slice_bitcast_fusion.1 = (bf16[512,4096]{0,1:T(8,128)(2,1)}, bf16[512,4096]{0,1:T(8,128)(2,1)}, bf16[512,4096]{0,1:T(8,128)(2,1)}) fusion(bf16[1,3,4096,512]{3,2,1,0:T(8,128)(2,1)} %param.27), kind=kLoop, calls=%fused_computation.19 | loop fusion | bytes 25165824 | tf_op jit(solution)/shard_map/dot_general | solution.py:113
  17.8 6.4 copy.294
  24.3 7.6 %dot_general.221 = bf16[4,64,2,4096]{3,2,1,0:T(2,128)(2,1)} reshape(bf16[512,4096]{1,0:T(8,128)(2,1)} %copy.294) | data formatting | bytes 8388608 | tf_op jit(solution)/shard_map/dot_general | solution.py:113
  31.9 6.4 copy.297
  38.4 6.5 copy.291
  44.8 7.6 %dot_general.217 = bf16[4,64,2,4096]{3,2,1,0:T(2,128)(2,1)} reshape(bf16[512,4096]{1,0:T(8,128)(2,1)} %copy.291) | data formatting | bytes 8388608 | tf_op jit(solution)/shard_map/dot_general | solution.py:109
  53.1 12.0 %fusion.262 = (bf16[1,1,64,512,128]{4,3,2,1,0:T(8,128)(2,1)}, bf16[1,1,64,512,128]{4,3,2,1,0:T(8,128)(2,1)}) fusion(bf16[1,2,64,512,128]{4,3,2,1,0:T(8,128)(2,1)} %param.29), kind=kLoop, calls=%fused_computation.419 | loop fusion | bytes 33554432 | tf_op jit(solution)/shard_map/slice | solution.py:97
  66.4 7.3 %fusion.28 = f32[64,4,64,2]{2,0,3,1:T(8,128)S(1)} fusion(bf16[4,64,2,4096]{3,2,1,0:T(2,128)(2,1)} %dot_general.217, f32[4096]{0:T(1024)S(1)} %bitcast.550, f32[64]{0:T(128)S(1)} %add_rsqrt_fusion.9, bf16[1,3,64,4096]{3,2,1,0:T(8,128)(2,1)} %all-gather.6.cloned.1.call-done), kind=kOutput, calls=%fused_computation.31 | convolution fusion | flops 269484032 | bytes 4866304 | tf_op jit(solution)/shard_map/dot_general | solution.py:109
  73.9 7.1 %fusion.22 = f32[64,4,64,2]{2,0,3,1:T(8,128)S(1)} fusion(bf16[4,64,2,4096]{3,2,1,0:T(2,128)(2,1)} %dot_general.221, f32[4096]{0:T(1024)S(1)} %bitcast.551, f32[64]{0:T(128)S(1)} %add_rsqrt_fusion.9, bf16[1,3,64,4096]{3,2,1,0:T(8,128)(2,1)S(1)} %copy-done.5), kind=kOutput, calls=%fused_computation.25 | convolution fusion | flops 269484032 | bytes 4866560 | tf_op jit(solution)/shard_map/dot_general | solution.py:113
  81.5 5.6 fusion.269
  87.6 19.6 %fusion.173 = f32[64,4,1,128]{3,2,1,0:T(1,128)S(1)} fusion(bf16[64,4,128,128]{3,2,1,0:T(8,128)(2,1)} %bitcast.520, bf16[64,4,128,1]{2,0,1,3:T(8,128)(2,1)S(1)} %fusion.197), kind=kOutput, calls=%fused_computation.254 | convolution fusion | flops 8388608 | bytes 8585216 | tf_op jit(solution)/shard_map/rhl,rhdl->rhd/dot_general | solution.py:132
  112.0 11.4 %copy.275 = bf16[512,8192]{1,0:T(8,128)(2,1)} copy(bf16[512,8192]{0,1:T(8,128)(2,1)} %bitcast.528) | data formatting | bytes 16777216 | tf_op jit(solution)/shard_map/dot_general | solution.py:161
  123.3 14.1 %dot_general.201 = bf16[8,32,2,8192]{3,2,1,0:T(2,128)(2,1)} reshape(bf16[512,8192]{1,0:T(8,128)(2,1)} %copy.275) | data formatting | bytes 16777216 | tf_op jit(solution)/shard_map/dot_general | solution.py:161
  141.9 61.5 %all-reduce.8.cloned.1.call-done = f32[64,4096]{1,0:T(8,128)} async-done(((f32[64,4096]{1,0:T(8,128)}), f32[64,4096]{1,0:T(8,128)}) %all-reduce.8.cloned.1.call-update) | async-done | bytes 1048592 | tf_op jit(solution)/shard_map/psum | solution.py:150
  205.6 7.2 %fusion.20 = f32[64,4,64,2]{2,0,3,1:T(8,128)S(1)} fusion(bf16[4,64,2,4096]{3,2,1,0:T(2,128)(2,1)} %dot_general.221, f32[64]{0:T(128)S(1)} %get-tuple-element.123, f32[4096]{0:T(1024)S(1)} %bitcast.553, bf16[1,3,64,4096]{3,2,1,0:T(8,128)(2,1)S(1)} %copy-done.5), kind=kOutput, calls=%fused_computation.23 | convolution fusion | flops 269484032 | bytes 4866560 | tf_op jit(solution)/shard_map/dot_general | solution.py:113
  212.9 5.1 fusion.26
  218.4 5.6 fusion.271
  224.7 7.2 %fusion.18 = f32[64,4,64,2]{2,0,3,1:T(8,128)S(1)} fusion(bf16[4,64,2,4096]{3,2,1,0:T(2,128)(2,1)} %dot_general.221, f32[64]{0:T(128)S(1)} %get-tuple-element.122, f32[4096]{0:T(1024)S(1)} %bitcast.555, bf16[1,3,64,4096]{3,2,1,0:T(8,128)(2,1)S(1)} %copy-done.5), kind=kOutput, calls=%fused_computation.21 | convolution fusion | flops 269484032 | bytes 4866560 | tf_op jit(solution)/shard_map/dot_general | solution.py:113
  232.0 5.1 fusion.24
  238.0 5.6 fusion.273
  244.7 3.7 fusion.66
  251.2 7.9 %fusion.169 = f32[64,4,1,128]{3,2,1,0:T(1,128)S(1)} fusion(bf16[64,4,128,128]{3,2,1,0:T(8,128)(2,1)} %bitcast.521, bf16[64,4,128,1]{2,0,1,3:T(8,128)(2,1)S(1)} %get-tuple-element.83), kind=kOutput, calls=%fused_computation.250 | convolution fusion | flops 8388608 | bytes 8585216 | tf_op jit(solution)/shard_map/rhl,rhdl->rhd/dot_general | solution.py:132
  259.6 4.4 fusion.171
  268.1 3.2 fusion.36
  271.9 9.5 %fusion.8 = f32[64,8,32,2]{0,2,3,1:T(8,128)S(1)} fusion(bf16[8,32,2,8192]{3,2,1,0:T(2,128)(2,1)} %dot_general.201, f32[64]{0:T(128)S(1)} %get-tuple-element.125, f32[8192]{0:T(1024)S(1)} %copy-done.49, bf16[3,64,8192]{2,1,0:T(8,128)(2,1)S(1)} %copy-done.4), kind=kOutput, calls=%fused_computation.8 | convolution fusion | flops 538968064 | bytes 9601536 | tf_op jit(solution)/shard_map/dot_general | solution.py:161
  300.1 9.4 %fusion.10 = f32[64,8,32,2]{0,2,3,1:T(8,128)S(1)} fusion(bf16[8,32,2,8192]{3,2,1,0:T(2,128)(2,1)} %dot_general.201, f32[8192]{0:T(1024)} %param.19, f32[64]{0:T(128)} %copy-done.52, bf16[3,64,8192]{2,1,0:T(8,128)(2,1)S(1)} %copy-done.4), kind=kOutput, calls=%fused_computation.10 | convolution fusion | flops 538968064 | bytes 9601280 | tf_op jit(solution)/shard_map/dot_general | solution.py:161
  318.0 9.0 %fusion.6 = f32[64,8,32,2]{0,2,3,1:T(8,128)S(1)} fusion(bf16[8,32,2,8192]{3,2,1,0:T(2,128)(2,1)} %dot_general.201, f32[64]{0:T(128)} %get-tuple-element.124, f32[8192]{0:T(1024)} %param.19, bf16[3,64,8192]{2,1,0:T(8,128)(2,1)S(1)} %copy-done.4), kind=kOutput, calls=%fused_computation.6 | convolution fusion | flops 538968064 | bytes 9601280 | tf_op jit(solution)/shard_map/dot_general | solution.py:161
  348.6 2.4 copy.312
  353.1 3.0 collective-permute-done.2
  364.7 2.6 fusion.94
  372.5 2.5 fusion.65
  381.6 6.5 fusion.272
  388.1 6.5 fusion.268
  394.6 2.9 fusion.270
  398.2 13.1 %fusion.51 = f32[1,64,2,1024]{3,1,0,2:T(8,128)} fusion(bf16[1,2,1024,4096]{3,2,1,0:T(8,128)(2,1)} %param.31, f32[64,4096]{1,0:T(8,128)} %all-reduce.8.cloned.1.call-done, f32[4096]{0:T(1024)S(1)} %bitcast.559, f32[64]{0:T(128)S(1)} %copy-done.44, bf16[1,3,64,4096]{3,2,1,0:T(8,128)(2,1)} %all-gather.6.cloned.1.call-done), kind=kOutput, calls=%fused_computation.72 | convolution fusion | flops 1075052544 | bytes 18891008 | tf_op jit(solution)/shard_map/dot_general | solution.py:153
  411.2 2.3 multiply_reduce_fusion.4
  413.5 12.8 %fusion.57 = f32[1,64,2,1024]{3,1,0,2:T(8,128)} fusion(bf16[1,2,1024,4096]{3,2,1,0:T(8,128)(2,1)} %param.31, f32[64,4096]{1,0:T(8,128)} %get-tuple-element.38, f32[64]{0:T(128)S(1)} %add_rsqrt_fusion, f32[4096]{0:T(1024)S(1)} %bitcast.560, bf16[1,3,64,4096]{3,2,1,0:T(8,128)(2,1)} %all-gather.6.cloned.1.call-done), kind=kOutput, calls=%fused_computation.74 | convolution fusion | flops 1075052544 | bytes 18891008 | tf_op jit(solution)/shard_map/dot_general | solution.py:153
  426.4 4.2 all-to-all-start.2
  430.6 12.6 %fusion.54 = f32[1,64,2,1024]{3,1,0,2:T(8,128)} fusion(bf16[1,2,1024,4096]{3,2,1,0:T(8,128)(2,1)} %param.31, f32[64,4096]{1,0:T(8,128)} %get-tuple-element.39, f32[64]{0:T(128)S(1)} %add_rsqrt_fusion.4, f32[4096]{0:T(1024)S(1)} %bitcast.561, bf16[1,3,64,4096]{3,2,1,0:T(8,128)(2,1)} %all-gather.6.cloned.1.call-done), kind=kOutput, calls=%fused_computation.73 | convolution fusion | flops 1075052544 | bytes 18891008 | tf_op jit(solution)/shard_map/dot_general | solution.py:153
  443.2 92.3 %all-reduce.10.cloned.1.call-done = (f32[64,8192]{1,0:T(8,128)}, f32[64,8192]{1,0:T(8,128)}, f32[64,8192]{1,0:T(8,128)}) async-done(((f32[64,8192]{1,0:T(8,128)}, f32[64,8192]{1,0:T(8,128)}, f32[64,8192]{1,0:T(8,128)}), (f32[64,8192]{1,0:T(8,128)}, f32[64,8192]{1,0:T(8,128)}, f32[64,8192]{1,0:T(8,128)})) %all-reduce.10.cloned.1.call-update) | async-done | bytes 6291472 | tf_op jit(solution)/shard_map/psum | solution.py:194
  535.5 3.9 multiply_reduce_fusion.2
  539.4 4.2 all-to-all-start.1
  543.7 11.7 %fusion.265 = (f32[64]{0:T(128)S(1)}, f32[64,1024]{1,0:T(8,128)S(1)}) fusion(f32[2,1,64,1,1024]{4,2,3,1,0:T(8,128)} %bitcast.128, bf16[1024,8192]{1,0:T(8,128)(2,1)} %param.25, f32[64,8192]{1,0:T(8,128)} %get-tuple-element.32, f32[64]{0:T(128)S(1)} %add_rsqrt_fusion.2, f32[8192]{0:T(1024)S(1)} %copy-done.15, bf16[3,64,8192]{2,1,0:T(8,128)(2,1)S(1)} %copy-done.4), kind=kOutput, calls=%fused_computation.422 | convolution fusion | flops 1076559872 | bytes 20742912 | tf_op jit(solution)/shard_map/dot_general | solution.py:197
  555.4 4.5 all-to-all-start
  559.9 12.4 %fusion.266 = (f32[64]{0:T(128)S(1)}, f32[64,1024]{1,0:T(8,128)}) fusion(f32[2,1,64,1,1024]{4,2,3,1,0:T(8,128)} %bitcast.92, bf16[1024,8192]{1,0:T(8,128)(2,1)} %param.25, f32[64,8192]{1,0:T(8,128)} %get-tuple-element.34, f32[64]{0:T(128)S(1)} %add_rsqrt_fusion.6, f32[8192]{0:T(1024)S(1)} %copy-done.15, bf16[3,64,8192]{2,1,0:T(8,128)(2,1)S(1)} %copy-done.4), kind=kOutput, calls=%fused_computation.423 | convolution fusion | flops 1076559872 | bytes 20742912 | tf_op jit(solution)/shard_map/dot_general | solution.py:197
  572.4 12.5 %fusion.267 = (f32[64]{0:T(128)S(1)}, f32[64,1024]{1,0:T(8,128)}) fusion(f32[2,1,64,1,1024]{4,2,3,1,0:T(8,128)} %bitcast.52, bf16[1024,8192]{1,0:T(8,128)(2,1)} %param.25, f32[64,8192]{1,0:T(8,128)} %get-tuple-element.33, f32[8192]{0:T(1024)S(1)} %copy-done.15, f32[64]{0:T(128)S(1)} %add_rsqrt_fusion.10, bf16[3,64,8192]{2,1,0:T(8,128)(2,1)S(1)} %copy-done.4), kind=kOutput, calls=%fused_computation.424 | convolution fusion | flops 1076559872 | bytes 20742912 | tf_op jit(solution)/shard_map/dot_general | solution.py:197
  584.8 33.0 %all-reduce.2 = (f32[64]{0:T(128)S(1)}, f32[64]{0:T(128)S(1)}, f32[64]{0:T(128)S(1)}) all-reduce(f32[64]{0:T(128)S(1)} %get-tuple-element.116, f32[64]{0:T(128)S(1)} %get-tuple-element.118, f32[64]{0:T(128)S(1)} %get-tuple-element.120), channel_id=1, replica_groups=mesh['grp'=2,'tp'=8,'dp'=2] {'grp','tp'}, use_global_device_ids=true, to_apply=%region_47.48 | all-reduce | flops 192 | bytes 1536 | tf_op jit(solution)/shard_map/pmax | solution.py:205
  620.4 29.5 %all-reduce = (f32[64]{0:T(128)S(1)}, f32[64]{0:T(128)S(1)}, f32[64]{0:T(128)S(1)}, f32[64]{0:T(128)S(1)}, f32[64]{0:T(128)S(1)}, /*index=5*/f32[64]{0:T(128)S(1)}) all-reduce(f32[64]{0:T(128)S(1)} %get-tuple-element.18, f32[64]{0:T(128)S(1)} %get-tuple-element.16, ...), channel_id=1, replica_groups=mesh['grp'=2,'tp'=8,'dp'=2] {'grp','tp'}, use_global_device_ids=true, to_apply=%region_49.50 | all-reduce | flops 384 | bytes 3072 | tf_op jit(solution)/shard_map/psum | solution.py:206
  (307 shorter events, 103.3 us)
Async XLA Ops:
  8.0 57.1 %all-gather.6.cloned.1.call-start = ((), (), s32[]{:S(2)}) async-start(), calls=%async_computation.5 | async-start | bytes 1769472 | tf_op jit(solution)/shard_map/all_gather | solution.py:93
  8.7 194.6 %all-reduce.8.cloned.1.call-start = ((), (), s32[]{:S(2)}) async-start(), calls=%async_computation.4 | async-start | bytes 2097152 | tf_op jit(solution)/shard_map/psum | solution.py:150
  44.8 7.6 %copy-start.42 = (s32[64]{0:T(128)S(1)}, s32[64]{0:T(128)}, u32[]{:S(2)}) copy-start(s32[64]{0:T(128)} %param.32) | copy-start | bytes 772
  52.6 84.9 %copy-start.27 = (f32[64]{0:T(128)}, f32[64]{0:T(128)S(1)}, u32[]{:S(2)}) copy-start(f32[64]{0:T(128)S(1)} %get-tuple-element.109) | copy-start | bytes 772
  52.6 84.9 %copy-start.29 = (f32[64]{0:T(128)}, f32[64]{0:T(128)S(1)}, u32[]{:S(2)}) copy-start(f32[64]{0:T(128)S(1)} %get-tuple-element.110) | copy-start | bytes 772
  52.6 84.9 %copy-start.31 = (f32[64]{0:T(128)}, f32[64]{0:T(128)S(1)}, u32[]{:S(2)}) copy-start(f32[64]{0:T(128)S(1)} %get-tuple-element.111) | copy-start | bytes 772
  53.1 13.3 %copy-start.16 = (f32[1,4096]{1,0:T(1,128)S(1)}, f32[1,4096]{1,0:T(1,128)}, u32[]{:S(2)}) copy-start(f32[1,4096]{1,0:T(1,128)} %param.26) | copy-start | bytes 49156
  66.4 7.6 %copy-start.5 = (bf16[1,3,64,4096]{3,2,1,0:T(8,128)(2,1)S(1)}, bf16[1,3,64,4096]{3,2,1,0:T(8,128)(2,1)}, u32[]{:S(2)}) copy-start(bf16[1,3,64,4096]{3,2,1,0:T(8,128)(2,1)} %all-gather.6.cloned.1.call-done) | copy-start | bytes 4718596
  87.6 19.6 %copy-start = (bf16[512,4096]{1,0:T(8,128)(2,1)S(1)}, bf16[512,4096]{1,0:T(8,128)(2,1)}, u32[]{:S(2)}) copy-start(bf16[512,4096]{1,0:T(8,128)(2,1)} %copy.297) | copy-start | bytes 12582916
  111.3 156.8 %all-gather.4.cloned.1.call-start = ((), (), s32[]{:S(2)}) async-start(), calls=%async_computation.3 | async-start | bytes 3342336 | tf_op jit(solution)/shard_map/all_gather | solution.py:92
  111.9 299.3 %all-reduce.12.cloned.1.call-start = ((), (), s32[]{:S(2)}) async-start(), calls=%async_computation.7 | async-start | bytes 4194304 | tf_op jit(solution)/shard_map/psum | solution.py:150
  137.5 68.0 %copy-start.33 = (f32[32]{0:T(128)}, f32[32]{0:T(128)S(1)}, u32[]{:S(2)}) copy-start(f32[32]{0:T(128)S(1)} %multiply_exponential_fusion.1) | copy-start | bytes 388
  205.6 7.3 %copy-start.40 = (f32[64]{0:T(128)}, f32[64]{0:T(128)S(1)}, u32[]{:S(2)}) copy-start(f32[64]{0:T(128)S(1)} %get-tuple-element.123) | copy-start | bytes 772
  205.6 26.4 %copy-start.38 = (f32[64]{0:T(128)}, f32[64]{0:T(128)S(1)}, u32[]{:S(2)}) copy-start(f32[64]{0:T(128)S(1)} %get-tuple-element.122) | copy-start | bytes 772
  205.6 7.3 %copy-start.10 = (bf16[4,64,2,4096]{3,2,1,0:T(2,128)(2,1)S(1)}, bf16[4,64,2,4096]{3,2,1,0:T(2,128)(2,1)}, u32[]{:S(2)}) copy-start(bf16[4,64,2,4096]{3,2,1,0:T(2,128)(2,1)} %dot_general.217) | copy-start | bytes 12582916
  224.7 7.3 %copy-start.11 = (bf16[4,64,2,4096]{3,2,1,0:T(2,128)(2,1)S(1)}, bf16[4,64,2,4096]{3,2,1,0:T(2,128)(2,1)}, u32[]{:S(2)}) copy-start(bf16[4,64,2,4096]{3,2,1,0:T(2,128)(2,1)} %dot_general.217) | copy-start | bytes 12582916
  238.0 6.7 %copy-start.41 = (f32[64]{0:T(128)S(1)}, f32[64]{0:T(128)}, u32[]{:S(2)}) copy-start(f32[64]{0:T(128)} %copy-done.40) | copy-start | bytes 772
  243.7 4.8 copy-start.39
  248.5 11.1 %slice-start.2 = ((s8[8388608]{0:T(1024)(128)(4,1)}), s8[4194304]{0:T(1024)(128)(4,1)S(1)}, s32[]{:S(2)}) async-start(s8[8388608]{0:T(1024)(128)(4,1)} %bitcast.522), calls=%async_computation.10 | async-start | bytes 8388608
  251.2 8.4 %slice-start.3 = ((s8[8388608]{0:T(1024)(128)(4,1)}), s8[4194304]{0:T(1024)(128)(4,1)S(1)}, s32[]{:S(2)}) async-start(s8[8388608]{0:T(1024)(128)(4,1)} %bitcast.522), calls=%async_computation.11 | async-start | bytes 8388608
  259.6 4.5 copy-start.3
  267.8 4.2 copy-start.49
  267.8 267.7 %all-reduce.10.cloned.1.call-start = ((), (), s32[]{:S(2)}) async-start(), calls=%async_computation.6 | async-start | bytes 12582912 | tf_op jit(solution)/shard_map/psum | solution.py:194
  271.9 9.5 %copy-start.46 = (f32[64]{0:T(128)}, f32[64]{0:T(128)S(1)}, u32[]{:S(2)}) copy-start(f32[64]{0:T(128)S(1)} %get-tuple-element.125) | copy-start | bytes 772
  281.8 5.1 copy-start.45
  281.8 5.6 copy-start.50
  284.2 5.5 copy-start.28
  298.1 50.6 %collective-permute-start.1 = (f32[64,8,130]{2,1,0:T(8,128)}, f32[64,8,130]{2,1,0:T(8,128)}, u32[]{:S(2)}, u32[]{:S(2)}) collective-permute-start(f32[64,8,130]{2,1,0:T(8,128)} %copy.311), channel_id=1, source_target_pairs={{0,2},{2,0},{4,6},{6,4},{8,10},{10,8},{12,14},{14,12},{1,3},{3,1},... | collective-permute-start | bytes 798728 | tf_op jit(solution)/shard_map/ppermute | solution.py:15
  300.1 9.4 %copy-start.22 = (f32[64,32]{0,1:T(8,128)S(1)}, f32[64,32]{0,1:T(8,128)}, u32[]{:S(2)}) copy-start(f32[64,32]{0,1:T(8,128)} %get-tuple-element.95) | copy-start | bytes 24580
  300.1 9.4 %copy-start.23 = (f32[64,32]{0,1:T(8,128)S(1)}, f32[64,32]{0,1:T(8,128)}, u32[]{:S(2)}) copy-start(f32[64,32]{0,1:T(8,128)} %get-tuple-element.96) | copy-start | bytes 24580
  317.3 9.7 %copy-start.20 = (f32[64,32]{0,1:T(8,128)S(1)}, f32[64,32]{0,1:T(8,128)}, u32[]{:S(2)}) copy-start(f32[64,32]{0,1:T(8,128)} %get-tuple-element.107) | copy-start | bytes 24580
  317.3 9.8 %copy-start.21 = (f32[64,32]{0,1:T(8,128)S(1)}, f32[64,32]{0,1:T(8,128)}, u32[]{:S(2)}) copy-start(f32[64,32]{0,1:T(8,128)} %get-tuple-element.108) | copy-start | bytes 24580
  317.3 27.0 %collective-permute-start = (f32[64,8,129]{2,1,0:T(8,128)}, f32[64,8,129]{2,1,0:T(8,128)}, u32[]{:S(2)}, u32[]{:S(2)}) collective-permute-start(f32[64,8,129]{2,1,0:T(8,128)} %copy.282), channel_id=1, source_target_pairs={{0,2},{2,0},{4,6},{6,4},{8,10},{10,8},{12,14},{14,12},{1,3},{3,1},... | collective-permute-start | bytes 792584 | tf_op jit(solution)/shard_map/ppermute | solution.py:15
  333.1 8.3 %copy-start.51 = (f32[8192]{0:T(1024)S(1)}, f32[8192]{0:T(1024)}, u32[]{:S(2)}) copy-start(f32[8192]{0:T(1024)} %param.19) | copy-start | bytes 98308
  333.1 8.3 %copy-start.53 = (f32[64]{0:T(128)S(1)}, f32[64]{0:T(128)}, u32[]{:S(2)}) copy-start(f32[64]{0:T(128)} %copy-done.52) | copy-start | bytes 772
  338.3 4.3 copy-start.47
  338.3 17.8 %collective-permute-start.2 = (f32[64,8,131]{2,1,0:T(8,128)}, f32[64,8,131]{2,1,0:T(8,128)}, u32[]{:S(2)}, u32[]{:S(2)}) collective-permute-start(f32[64,8,131]{2,1,0:T(8,128)} %copy.333), channel_id=1, source_target_pairs={{0,2},{2,0},{4,6},{6,4},{8,10},{10,8},{12,14},{14,12},{1,3},{3,1},... | collective-permute-start | bytes 804872 | tf_op jit(solution)/shard_map/ppermute | solution.py:15
  342.6 8.5 %copy-start.19 = (f32[64,8,2]{0,1,2:T(8,128)S(1)}, f32[64,8,2]{0,1,2:T(8,128)}, u32[]{:S(2)}) copy-start(f32[64,8,2]{0,1,2:T(8,128)} %copy.310) | copy-start | bytes 12292
  381.6 6.5 copy-start.14
  381.6 13.0 %slice-start = ((s8[8388608]{0:T(1024)(128)(4,1)}), s8[4194304]{0:T(1024)(128)(4,1)S(1)}, s32[]{:S(2)}) async-start(s8[8388608]{0:T(1024)(128)(4,1)} %bitcast.518), calls=%async_computation.8 | async-start | bytes 8388608
  388.1 6.5 slice-start.1
  426.4 113.1 %all-to-all-start.2 = ((f32[1,64,2,1024]{3,1,0,2:T(8,128)}), f32[1,64,2,1024]{3,1,0,2:T(8,128)}, u32[]{:S(2)}, u32[]{:S(2)}) async-start(f32[1,64,2,1024]{3,1,0,2:T(8,128)} %fusion.57), calls=%async_computation.2 | async-start | bytes 1048576 | tf_op jit(solution)/shard_map/all_to_all | solution.py:157
  535.5 8.1 %copy-start.15 = (f32[8192]{0:T(1024)S(1)}, f32[8192]{0:T(1024)}, u32[]{:S(2)}) copy-start(f32[8192]{0:T(1024)} %param.24) | copy-start | bytes 98308
  539.4 16.0 %all-to-all-start.1 = ((f32[1,64,2,1024]{3,1,0,2:T(8,128)}), f32[1,64,2,1024]{3,1,0,2:T(8,128)}, u32[]{:S(2)}, u32[]{:S(2)}) async-start(f32[1,64,2,1024]{3,1,0,2:T(8,128)} %fusion.54), calls=%async_computation.1 | async-start | bytes 1048576 | tf_op jit(solution)/shard_map/all_to_all | solution.py:157
  555.4 16.9 %all-to-all-start = ((f32[1,64,2,1024]{3,1,0,2:T(8,128)}), f32[1,64,2,1024]{3,1,0,2:T(8,128)}, u32[]{:S(2)}, u32[]{:S(2)}) async-start(f32[1,64,2,1024]{3,1,0,2:T(8,128)} %fusion.51), calls=%async_computation | async-start | bytes 1048576 | tf_op jit(solution)/shard_map/all_to_all | solution.py:157
  572.3 45.5 %copy-start.37 = (s32[64]{0:T(128)S(1)}, s32[64]{0:T(128)}, u32[]{:S(2)}) copy-start(s32[64]{0:T(128)} %get-tuple-element.87) | copy-start | bytes 772
  572.3 45.7 %copy-start.36 = (s32[64]{0:T(128)S(1)}, s32[64]{0:T(128)}, u32[]{:S(2)}) copy-start(s32[64]{0:T(128)} %get-tuple-element.88) | copy-start | bytes 772
  572.3 46.9 %copy-start.35 = (s32[64]{0:T(128)S(1)}, s32[64]{0:T(128)}, u32[]{:S(2)}) copy-start(s32[64]{0:T(128)} %get-tuple-element.86) | copy-start | bytes 772
  (21 other events, 51.3 us)
Sparse Core Ops, SparseCore 0:
  10.8 47.1 all-gather.5
  111.4 91.8 all-reduce.7
  267.9 104.6 all-reduce.11
  397.6 137.8 all-reduce.9
Sparse Core Ops, SparseCore 1:
  113.9 52.9 all-gather.3
where the time goes:
time: 667 us; the launch traced here: 661 us
  matrix products  245 us (37%)
  waiting for transfers between devices  158 us (24%)
  local copies, waits for them, and re-layouts  118 us (18%)
  blocking collectives  62.5 us (9%)
  other arithmetic  43.7 us (7%)
  between operations  16.9 us (3%)
  starting transfers between devices  16.7 us (3%)
    psum x1, waiting for transfers between devices, body(): mixed_sum = lax.psum(partial_value, ('grp', 'tp'))  92.3 us
    psum x2, waiting for transfers between devices, body(): small_mixed = lax.psum(small_partial, 'tp')  61.5 us
    dot_general x3, matrix products, body(): lax.dot_general(small_final, small_table, (((1,), (1,)), ((), ())), prefe...  38.5 us
    dot_general x3, matrix products, body(): lax.dot_general(final_rows, base_unembed, (((1,), (1,)), ((), ())), prefe...  36.6 us
    pmax x1, blocking collectives, body(): row_max = lax.pmax(local_max, ('grp', 'tp'))  33 us
    dot_general x3, matrix products, body(): jnp.einsum('rhl,rhdl->rhd', small_cached_weights, small_values_cache, pre...  31.9 us
    psum x1, blocking collectives, body(): lax.psum((jnp.sum(jnp.exp(steered - row_max[:, None]), axis=-1), picked_l...  29.5 us
    dot_general x3, matrix products, body(): jnp.dot(normed, base_query, preferred_element_type=jnp.float32)  27.9 us
  transfers between devices with their start and end apart: 11, of which 3 were waited for; matrix products, arithmetic and copies ran while one was open for 51% of the time, Pallas kernels for 0%

commit v1 on v0

--- a/solution.py
+++ b/solution.py
@@ -147,7 +147,11 @@
         small_partial = jnp.dot(
             small_head_values, small_output[0], preferred_element_type=jnp.float32
         )
-        small_mixed = lax.psum(small_partial, "tp")
+        small_mixed = small_partial
+        for hop in (1, 2, 4):
+            small_mixed = small_mixed + lax.ppermute(
+                small_mixed, "tp", [(dev, dev ^ hop) for dev in range(8)]
+            )
         small_hidden = small_full[step_index].astype(jnp.float32) + small_mixed
         small_final = norm_rows(small_hidden, small_final_gain[0])
         small_logits = lax.dot_general(

time: 667 us -> 795 us (1.19)
  waiting for transfers between devices: 158 us -> 266 us
  starting transfers between devices: 16.7 us -> 27.9 us
    ppermute x0 -> x9, waiting for transfers between devices: none -> 207 us  [body(): lax.ppermute(small_mixed, 'tp', [(dev, dev ^ hop) for dev in range(8)])]
    psum x2 -> x0, waiting for transfers between devices: 61.5 us -> none  [body(): small_mixed = lax.psum(small_partial, 'tp')]
    psum x1, waiting for transfers between devices: 92.3 us -> 58.2 us  [body(): mixed_sum = lax.psum(partial_value, ('grp', 'tp'))]
    ppermute x0 -> x9, starting transfers between devices: none -> 11.6 us  [body(): lax.ppermute(small_mixed, 'tp', [(dev, dev ^ hop) for dev in range(8)])]
  transfers between devices with their start and end apart: 11 -> 18, of which waited for: 3 -> 8; matrix products, arithmetic and copies ran while one was open for 51% -> 44% of each run, Pallas kernels for 0% -> 0%
where the time goes in v1:
time: 795 us; the launch traced here: 789 us
  waiting for transfers between devices  266 us (33%)
  matrix products  246 us (31%)
  local copies, waits for them, and re-layouts  118 us (15%)
  blocking collectives  62.5 us (8%)
  other arithmetic  51.4 us (6%)
  starting transfers between devices  27.9 us (4%)
  between operations  17.2 us (2%)
    ppermute x9, waiting for transfers between devices, body(): lax.ppermute(small_mixed, 'tp', [(dev, dev ^ hop) for dev in range(8)])  207 us
    psum x1, waiting for transfers between devices, body(): mixed_sum = lax.psum(partial_value, ('grp', 'tp'))  58.2 us
    dot_general x3, matrix products, body(): lax.dot_general(small_final, small_table, (((1,), (1,)), ((), ())), prefe...  38.4 us
    dot_general x3, matrix products, body(): lax.dot_general(final_rows, base_unembed, (((1,), (1,)), ((), ())), prefe...  36.6 us
    dot_general x3, matrix products, body(): jnp.einsum('rhl,rhdl->rhd', small_cached_weights, small_values_cache, pre...  35.6 us
    pmax x1, blocking collectives, body(): row_max = lax.pmax(local_max, ('grp', 'tp'))  33 us
    psum x1, blocking collectives, body(): lax.psum((jnp.sum(jnp.exp(steered - row_max[:, None]), axis=-1), picked_l...  29.5 us
    dot_general x3, matrix products, body(): jnp.dot(normed, base_query, preferred_element_type=jnp.float32)  27.1 us
  transfers between devices with their start and end apart: 18, of which 8 were waited for; matrix products, arithmetic and copies ran while one was open for 44% of the time, Pallas kernels for 0%

profile of v1, /device:TPU:0, one launch (start us, length us, event | category | flops | bytes accessed | tf_op | source)
XLA Modules:
  0.0 788.5 jit_solution(14429133984878485804)
XLA Ops:
  8.8 9.1 %slice_bitcast_fusion.1 = (bf16[512,4096]{0,1:T(8,128)(2,1)}, bf16[512,4096]{0,1:T(8,128)(2,1)}, bf16[512,4096]{0,1:T(8,128)(2,1)}) fusion(bf16[1,3,4096,512]{3,2,1,0:T(8,128)(2,1)} %param.27), kind=kLoop, calls=%fused_computation.19 | loop fusion | bytes 25165824 | tf_op jit(solution)/shard_map/dot_general | solution.py:113
  17.8 6.4 copy.294
  24.3 7.6 dot_general.221
  31.9 6.4 copy.297
  38.4 6.5 copy.291
  44.9 7.6 dot_general.217
  53.1 12.0 %fusion.262 = (bf16[1,1,64,512,128]{4,3,2,1,0:T(8,128)(2,1)}, bf16[1,1,64,512,128]{4,3,2,1,0:T(8,128)(2,1)}) fusion(bf16[1,2,64,512,128]{4,3,2,1,0:T(8,128)(2,1)} %param.29), kind=kLoop, calls=%fused_computation.416 | loop fusion | bytes 33554432 | tf_op jit(solution)/shard_map/slice | solution.py:97
  66.4 7.3 fusion.28
  74.0 7.1 fusion.22
  81.5 5.6 fusion.269
  87.7 19.7 %fusion.170 = f32[64,4,1,128]{3,2,1,0:T(1,128)S(1)} fusion(bf16[64,4,128,128]{3,2,1,0:T(8,128)(2,1)} %bitcast.514, bf16[64,4,128,1]{2,0,1,3:T(8,128)(2,1)S(1)} %fusion.197), kind=kOutput, calls=%fused_computation.251 | convolution fusion | flops 8388608 | bytes 8585216 | tf_op jit(solution)/shard_map/rhl,rhdl->rhd/dot_general | solution.py:132
  113.5 23.2 %collective-permute-done.1 = f32[64,4096]{1,0:T(8,128)S(1)} collective-permute-done((f32[64,4096]{1,0:T(8,128)S(1)}, f32[64,4096]{1,0:T(8,128)S(1)}, u32[]{:S(2)}, u32[]{:S(2)}) %collective-permute-start.1) | collective-permute-done | bytes 1048608 | tf_op jit(solution)/shard_map/ppermute | solution.py:152
  138.8 28.9 %collective-permute-done.2 = f32[64,4096]{1,0:T(8,128)} collective-permute-done((f32[64,4096]{1,0:T(8,128)S(1)}, f32[64,4096]{1,0:T(8,128)}, u32[]{:S(2)}, u32[]{:S(2)}) %collective-permute-start.2) | collective-permute-done | bytes 1048608 | tf_op jit(solution)/shard_map/ppermute | solution.py:152
  173.0 11.4 %copy.275 = bf16[512,8192]{1,0:T(8,128)(2,1)} copy(bf16[512,8192]{0,1:T(8,128)(2,1)} %bitcast.520) | data formatting | bytes 16777216 | tf_op jit(solution)/shard_map/dot_general | solution.py:165
  184.4 14.1 %dot_general.201 = bf16[8,32,2,8192]{3,2,1,0:T(2,128)(2,1)} reshape(bf16[512,8192]{1,0:T(8,128)(2,1)} %copy.275) | data formatting | bytes 16777216 | tf_op jit(solution)/shard_map/dot_general | solution.py:165
  202.6 26.5 %collective-permute-done.3 = f32[64,4096]{1,0:T(8,128)} collective-permute-done((f32[64,4096]{1,0:T(8,128)S(1)}, f32[64,4096]{1,0:T(8,128)}, u32[]{:S(2)}, u32[]{:S(2)}) %collective-permute-start.3) | collective-permute-done | bytes 1048608 | tf_op jit(solution)/shard_map/ppermute | solution.py:152
  231.3 7.2 fusion.20
  238.6 5.1 fusion.26
  244.1 6.0 fusion.271
  250.3 7.2 fusion.18
  257.6 5.1 fusion.24
  263.6 5.8 fusion.273
  270.2 3.6 fusion.66
  274.5 7.9 %fusion.168 = f32[64,4,1,128]{3,2,1,0:T(1,128)S(1)} fusion(bf16[64,4,128,128]{3,2,1,0:T(8,128)(2,1)} %bitcast.515, bf16[64,4,128,1]{2,0,1,3:T(8,128)(2,1)S(1)} %get-tuple-element.81), kind=kOutput, calls=%fused_computation.249 | convolution fusion | flops 8388608 | bytes 8585216 | tf_op jit(solution)/shard_map/rhl,rhdl->rhd/dot_general | solution.py:132
  285.7 3.6 fusion.67
  289.7 7.9 %fusion.166 = f32[64,4,1,128]{3,2,1,0:T(1,128)S(1)} fusion(bf16[64,4,128,128]{3,2,1,0:T(8,128)(2,1)} %bitcast.516, bf16[64,4,128,1]{2,0,1,3:T(8,128)(2,1)S(1)} %get-tuple-element.80), kind=kOutput, calls=%fused_computation.247 | convolution fusion | flops 8388608 | bytes 8585216 | tf_op jit(solution)/shard_map/rhl,rhdl->rhd/dot_general | solution.py:132
  300.4 3.2 fusion.36
  304.3 9.2 %fusion.8 = f32[64,8,32,2]{0,2,3,1:T(8,128)S(1)} fusion(bf16[8,32,2,8192]{3,2,1,0:T(2,128)(2,1)} %dot_general.201, f32[64]{0:T(128)S(1)} %get-tuple-element.123, f32[8192]{0:T(1024)S(1)} %copy-done.51, bf16[3,64,8192]{2,1,0:T(8,128)(2,1)S(1)} %copy-done.4), kind=kOutput, calls=%fused_computation.8 | convolution fusion | flops 538968064 | bytes 9601536 | tf_op jit(solution)/shard_map/dot_general | solution.py:165
  331.9 9.0 %fusion.10 = f32[64,8,32,2]{0,2,3,1:T(8,128)S(1)} fusion(bf16[8,32,2,8192]{3,2,1,0:T(2,128)(2,1)} %dot_general.201, f32[8192]{0:T(1024)} %param.19, f32[64]{0:T(128)} %copy-done.54, bf16[3,64,8192]{2,1,0:T(8,128)(2,1)S(1)} %copy-done.4), kind=kOutput, calls=%fused_computation.10 | convolution fusion | flops 538968064 | bytes 9601280 | tf_op jit(solution)/shard_map/dot_general | solution.py:165
  349.9 9.0 %fusion.6 = f32[64,8,32,2]{0,2,3,1:T(8,128)S(1)} fusion(bf16[8,32,2,8192]{3,2,1,0:T(2,128)(2,1)} %dot_general.201, f32[64]{0:T(128)} %get-tuple-element.122, f32[8192]{0:T(1024)} %param.19, bf16[3,64,8192]{2,1,0:T(8,128)(2,1)S(1)} %copy-done.4), kind=kOutput, calls=%fused_computation.6 | convolution fusion | flops 538968064 | bytes 9601280 | tf_op jit(solution)/shard_map/dot_general | solution.py:165
  415.7 6.2 fusion.272
  424.9 24.2 %collective-permute-done.6 = f32[64,4096]{1,0:T(8,128)S(1)} collective-permute-done((f32[64,4096]{1,0:T(8,128)S(1)}, f32[64,4096]{1,0:T(8,128)S(1)}, u32[]{:S(2)}, u32[]{:S(2)}) %collective-permute-start.6) | collective-permute-done | bytes 1048608 | tf_op jit(solution)/shard_map/ppermute | solution.py:152
  450.2 21.6 %collective-permute-done.10 = f32[64,4096]{1,0:T(8,128)S(1)} collective-permute-done((f32[64,4096]{1,0:T(8,128)S(1)}, f32[64,4096]{1,0:T(8,128)S(1)}, u32[]{:S(2)}, u32[]{:S(2)}) %collective-permute-start.10) | collective-permute-done | bytes 1048608 | tf_op jit(solution)/shard_map/ppermute | solution.py:152
  476.6 12.6 %fusion.51 = f32[1,64,2,1024]{3,1,0,2:T(8,128)} fusion(bf16[1,2,1024,4096]{3,2,1,0:T(8,128)(2,1)} %param.31, f32[4096]{0:T(1024)S(1)} %bitcast.551, f32[64]{0:T(128)S(1)} %copy-done.46, f32[64,4096]{1,0:T(8,128)} %copy-done.6, f32[64,4096]{1,0:T(8,128)} %collective-permute-done.3, bf16[1,3,64,4096]{3,2,1,0:T(8,128)(2,1)} %all-gather.6.cloned.1.call-done), kind=kOutput, calls=%fused_computation.72 | convolution fusion | flops 1075314688 | bytes 19939584 | tf_op jit(solution)/shard_map/dot_general | solution.py:157
  489.2 45.1 %collective-permute-done.7 = f32[64,4096]{1,0:T(8,128)} collective-permute-done((f32[64,4096]{1,0:T(8,128)}, f32[64,4096]{1,0:T(8,128)}, u32[]{:S(2)}, u32[]{:S(2)}) %collective-permute-start.7) | collective-permute-done | bytes 1048608 | tf_op jit(solution)/shard_map/ppermute | solution.py:152
  534.3 37.2 %collective-permute-done.11 = f32[64,4096]{1,0:T(8,128)} collective-permute-done((f32[64,4096]{1,0:T(8,128)}, f32[64,4096]{1,0:T(8,128)}, u32[]{:S(2)}, u32[]{:S(2)}) %collective-permute-start.11) | collective-permute-done | bytes 1048608 | tf_op jit(solution)/shard_map/ppermute | solution.py:152
  574.5 13.1 %fusion.57 = f32[1,64,2,1024]{3,1,0,2:T(8,128)} fusion(bf16[1,2,1024,4096]{3,2,1,0:T(8,128)(2,1)} %param.31, f32[64]{0:T(128)S(1)} %add_rsqrt_fusion, f32[4096]{0:T(1024)S(1)} %bitcast.552, f32[64,4096]{1,0:T(8,128)} %add.401, f32[64,4096]{1,0:T(8,128)} %collective-permute-done.11, bf16[1,3,64,4096]{3,2,1,0:T(8,128)(2,1)} %all-gather.6.cloned.1.call-done), kind=kOutput, calls=%fused_computation.74 | convolution fusion | flops 1075314688 | bytes 19939584 | tf_op jit(solution)/shard_map/dot_general | solution.py:157
  587.6 4.2 all-to-all-start.2
  591.9 12.7 %fusion.54 = f32[1,64,2,1024]{3,1,0,2:T(8,128)} fusion(bf16[1,2,1024,4096]{3,2,1,0:T(8,128)(2,1)} %param.31, f32[64]{0:T(128)S(1)} %add_rsqrt_fusion.4, f32[4096]{0:T(1024)S(1)} %bitcast.553, f32[64,4096]{1,0:T(8,128)} %add.379, f32[64,4096]{1,0:T(8,128)} %collective-permute-done.7, bf16[1,3,64,4096]{3,2,1,0:T(8,128)(2,1)} %all-gather.6.cloned.1.call-done), kind=kOutput, calls=%fused_computation.73 | convolution fusion | flops 1075314688 | bytes 19939584 | tf_op jit(solution)/shard_map/dot_general | solution.py:157
  604.6 58.2 %all-reduce.5.cloned.1.call-done = (f32[64,8192]{1,0:T(8,128)}, f32[64,8192]{1,0:T(8,128)}, f32[64,8192]{1,0:T(8,128)}) async-done(((f32[64,8192]{1,0:T(8,128)}, f32[64,8192]{1,0:T(8,128)}, f32[64,8192]{1,0:T(8,128)}), (f32[64,8192]{1,0:T(8,128)}, f32[64,8192]{1,0:T(8,128)}, f32[64,8192]{1,0:T(8,128)})) %all-reduce.5.cloned.1.call-update) | async-done | bytes 6291472 | tf_op jit(solution)/shard_map/psum | solution.py:198
  662.8 3.9 multiply_reduce_fusion.2
  666.7 4.2 all-to-all-start.1
  670.9 11.7 %fusion.265 = (f32[64]{0:T(128)S(1)}, f32[64,1024]{1,0:T(8,128)S(1)}) fusion(f32[2,1,64,1,1024]{4,2,3,1,0:T(8,128)} %bitcast.128, bf16[1024,8192]{1,0:T(8,128)(2,1)} %param.25, f32[64,8192]{1,0:T(8,128)} %get-tuple-element.32, f32[64]{0:T(128)S(1)} %add_rsqrt_fusion.2, f32[8192]{0:T(1024)S(1)} %copy-done.19, bf16[3,64,8192]{2,1,0:T(8,128)(2,1)S(1)} %copy-done.4), kind=kOutput, calls=%fused_computation.419 | convolution fusion | flops 1076559872 | bytes 20742912 | tf_op jit(solution)/shard_map/dot_general | solution.py:201
  682.7 4.5 all-to-all-start
  687.2 12.4 %fusion.266 = (f32[64]{0:T(128)S(1)}, f32[64,1024]{1,0:T(8,128)}) fusion(f32[2,1,64,1,1024]{4,2,3,1,0:T(8,128)} %bitcast.92, bf16[1024,8192]{1,0:T(8,128)(2,1)} %param.25, f32[64,8192]{1,0:T(8,128)} %get-tuple-element.34, f32[64]{0:T(128)S(1)} %add_rsqrt_fusion.6, f32[8192]{0:T(1024)S(1)} %copy-done.19, bf16[3,64,8192]{2,1,0:T(8,128)(2,1)S(1)} %copy-done.4), kind=kOutput, calls=%fused_computation.420 | convolution fusion | flops 1076559872 | bytes 20742912 | tf_op jit(solution)/shard_map/dot_general | solution.py:201
  699.6 12.4 %fusion.267 = (f32[64]{0:T(128)S(1)}, f32[64,1024]{1,0:T(8,128)}) fusion(f32[2,1,64,1,1024]{4,2,3,1,0:T(8,128)} %bitcast.52, bf16[1024,8192]{1,0:T(8,128)(2,1)} %param.25, f32[64,8192]{1,0:T(8,128)} %get-tuple-element.33, f32[8192]{0:T(1024)S(1)} %copy-done.19, f32[64]{0:T(128)S(1)} %add_rsqrt_fusion.10, bf16[3,64,8192]{2,1,0:T(8,128)(2,1)S(1)} %copy-done.4), kind=kOutput, calls=%fused_computation.421 | convolution fusion | flops 1076559872 | bytes 20742912 | tf_op jit(solution)/shard_map/dot_general | solution.py:201
  712.1 33.0 %all-reduce.2 = (f32[64]{0:T(128)S(1)}, f32[64]{0:T(128)S(1)}, f32[64]{0:T(128)S(1)}) all-reduce(f32[64]{0:T(128)S(1)} %get-tuple-element.114, f32[64]{0:T(128)S(1)} %get-tuple-element.116, f32[64]{0:T(128)S(1)} %get-tuple-element.118), channel_id=1, replica_groups=mesh['grp'=2,'tp'=8,'dp'=2] {'grp','tp'}, use_global_device_ids=true, to_apply=%region_44.45 | all-reduce | flops 192 | bytes 1536 | tf_op jit(solution)/shard_map/pmax | solution.py:209
  747.7 29.5 %all-reduce = (f32[64]{0:T(128)S(1)}, f32[64]{0:T(128)S(1)}, f32[64]{0:T(128)S(1)}, f32[64]{0:T(128)S(1)}, f32[64]{0:T(128)S(1)}, /*index=5*/f32[64]{0:T(128)S(1)}) all-reduce(f32[64]{0:T(128)S(1)} %get-tuple-element.18, f32[64]{0:T(128)S(1)} %get-tuple-element.16, ...), channel_id=1, replica_groups=mesh['grp'=2,'tp'=8,'dp'=2] {'grp','tp'}, use_global_device_ids=true, to_apply=%region_46.47 | all-reduce | flops 384 | bytes 3072 | tf_op jit(solution)/shard_map/psum | solution.py:210
  (324 shorter events, 135.1 us)
Async XLA Ops:
  8.0 57.1 %all-gather.6.cloned.1.call-start = ((), (), s32[]{:S(2)}) async-start(), calls=%async_computation.4 | async-start | bytes 1769472 | tf_op jit(solution)/shard_map/all_gather | solution.py:93
  8.7 291.7 %all-gather.4.cloned.1.call-start = ((), (), s32[]{:S(2)}) async-start(), calls=%async_computation.3 | async-start | bytes 3342336 | tf_op jit(solution)/shard_map/all_gather | solution.py:92
  44.9 7.6 copy-start.44
  52.6 149.1 %copy-start.31 = (f32[64]{0:T(128)}, f32[64]{0:T(128)S(1)}, u32[]{:S(2)}) copy-start(f32[64]{0:T(128)S(1)} %get-tuple-element.107) | copy-start | bytes 772
  52.6 149.1 %copy-start.33 = (f32[64]{0:T(128)}, f32[64]{0:T(128)S(1)}, u32[]{:S(2)}) copy-start(f32[64]{0:T(128)S(1)} %get-tuple-element.108) | copy-start | bytes 772
  52.6 149.1 %copy-start.35 = (f32[64]{0:T(128)}, f32[64]{0:T(128)S(1)}, u32[]{:S(2)}) copy-start(f32[64]{0:T(128)S(1)} %get-tuple-element.109) | copy-start | bytes 772
  53.1 13.3 %copy-start.20 = (f32[1,4096]{1,0:T(1,128)S(1)}, f32[1,4096]{1,0:T(1,128)}, u32[]{:S(2)}) copy-start(f32[1,4096]{1,0:T(1,128)} %param.26) | copy-start | bytes 49156
  66.4 7.6 copy-start.5
  87.6 19.7 %copy-start = (bf16[512,4096]{1,0:T(8,128)(2,1)S(1)}, bf16[512,4096]{1,0:T(8,128)(2,1)}, u32[]{:S(2)}) copy-start(bf16[512,4096]{1,0:T(8,128)(2,1)} %copy.297) | copy-start | bytes 12582916
  110.5 26.2 %collective-permute-start.1 = (f32[64,4096]{1,0:T(8,128)S(1)}, f32[64,4096]{1,0:T(8,128)S(1)}, u32[]{:S(2)}, u32[]{:S(2)}) collective-permute-start(f32[64,4096]{1,0:T(8,128)S(1)} %fusion.16), channel_id=1, source_target_pairs={{0,2},{2,0},{4,6},{6,4},{8,10},{10,8},{12,14},{14,12},{1,3},{3,1},... | collective-permute-start | bytes 3145736 | tf_op jit(solution)/shard_map/ppermute | solution.py:152
  136.9 30.8 %collective-permute-start.2 = (f32[64,4096]{1,0:T(8,128)S(1)}, f32[64,4096]{1,0:T(8,128)}, u32[]{:S(2)}, u32[]{:S(2)}) collective-permute-start(f32[64,4096]{1,0:T(8,128)S(1)} %add.356), channel_id=1, source_target_pairs={{0,4},{2,6},{4,0},{6,2},{8,12},{10,14},{12,8},{14,10},{1,5},{3,7},... | collective-permute-start | bytes 3145736 | tf_op jit(solution)/shard_map/ppermute | solution.py:152
  138.7 524.0 %all-reduce.5.cloned.1.call-start = ((), (), s32[]{:S(2)}) async-start(), calls=%async_computation.5 | async-start | bytes 12582912 | tf_op jit(solution)/shard_map/psum | solution.py:198
  138.8 33.1 %copy-start.15 = (bf16[2,8192,64]{1,2,0:T(8,128)(2,1)S(1)}, bf16[2,8192,64]{1,2,0:T(8,128)(2,1)}, u32[]{:S(2)}) copy-start(bf16[2,8192,64]{1,2,0:T(8,128)(2,1)} %param.21) | copy-start | bytes 6291460
  169.4 59.6 %copy-start.6 = (f32[64,4096]{1,0:T(8,128)}, f32[64,4096]{1,0:T(8,128)S(1)}, u32[]{:S(2)}) copy-start(f32[64,4096]{1,0:T(8,128)S(1)} %add.357) | copy-start | bytes 3145732
  169.5 59.6 %collective-permute-start.3 = (f32[64,4096]{1,0:T(8,128)S(1)}, f32[64,4096]{1,0:T(8,128)}, u32[]{:S(2)}, u32[]{:S(2)}) collective-permute-start(f32[64,4096]{1,0:T(8,128)S(1)} %add.357), channel_id=1, source_target_pairs={{0,8},{2,10},{4,12},{6,14},{8,0},{10,2},{12,4},{14,6},{1,9},{3,11}... | collective-permute-start | bytes 3145736 | tf_op jit(solution)/shard_map/ppermute | solution.py:152
  184.4 16.7 %copy-start.45 = (s32[3,64]{1,0:T(4,128)S(1)}, s32[3,64]{1,0:T(4,128)}, u32[]{:S(2)}) copy-start(s32[3,64]{1,0:T(4,128)} %param.33) | copy-start | bytes 2308
  201.1 37.5 %copy-start.37 = (f32[32]{0:T(128)}, f32[32]{0:T(128)S(1)}, u32[]{:S(2)}) copy-start(f32[32]{0:T(128)S(1)} %multiply_exponential_fusion.1) | copy-start | bytes 388
  231.3 7.3 copy-start.42
  231.3 7.3 copy-start.12
  274.5 8.0 %copy-start.2 = (bf16[1,512,4096]{2,1,0:T(8,128)(2,1)S(1)}, bf16[1,512,4096]{2,1,0:T(8,128)(2,1)}, u32[]{:S(2)}) copy-start(bf16[1,512,4096]{2,1,0:T(8,128)(2,1)} %param.28) | copy-start | bytes 12582916
  284.3 125.7 %collective-permute-start.5 = (f32[64,4096]{1,0:T(8,128)}, f32[64,4096]{1,0:T(8,128)}, u32[]{:S(2)}, u32[]{:S(2)}) collective-permute-start(f32[64,4096]{1,0:T(8,128)} %fusion.14), channel_id=1, source_target_pairs={{0,2},{2,0},{4,6},{6,4},{8,10},{10,8},{12,14},{14,12},{1,3},{3,1},... | collective-permute-start | bytes 3145736 | tf_op jit(solution)/shard_map/ppermute | solution.py:152
  289.7 8.0 %copy-start.3 = (bf16[1,512,4096]{2,1,0:T(8,128)(2,1)S(1)}, bf16[1,512,4096]{2,1,0:T(8,128)(2,1)}, u32[]{:S(2)}) copy-start(bf16[1,512,4096]{2,1,0:T(8,128)(2,1)} %param.28) | copy-start | bytes 12582916
  299.6 112.2 %collective-permute-start.9 = (f32[64,4096]{1,0:T(8,128)}, f32[64,4096]{1,0:T(8,128)}, u32[]{:S(2)}, u32[]{:S(2)}) collective-permute-start(f32[64,4096]{1,0:T(8,128)} %fusion.12), channel_id=1, source_target_pairs={{0,2},{2,0},{4,6},{6,4},{8,10},{10,8},{12,14},{14,12},{1,3},{3,1},... | collective-permute-start | bytes 3145736 | tf_op jit(solution)/shard_map/ppermute | solution.py:152
  304.3 9.2 %copy-start.50 = (f32[64]{0:T(128)}, f32[64]{0:T(128)S(1)}, u32[]{:S(2)}) copy-start(f32[64]{0:T(128)S(1)} %get-tuple-element.123) | copy-start | bytes 772
  330.0 50.7 %collective-permute-start.4 = (f32[64,8,130]{2,1,0:T(8,128)}, f32[64,8,130]{2,1,0:T(8,128)}, u32[]{:S(2)}, u32[]{:S(2)}) collective-permute-start(f32[64,8,130]{2,1,0:T(8,128)} %copy.311), channel_id=1, source_target_pairs={{0,2},{2,0},{4,6},{6,4},{8,10},{10,8},{12,14},{14,12},{1,3},{3,1},... | collective-permute-start | bytes 798728 | tf_op jit(solution)/shard_map/ppermute | solution.py:15
  331.9 9.0 %copy-start.26 = (f32[64,32]{0,1:T(8,128)S(1)}, f32[64,32]{0,1:T(8,128)}, u32[]{:S(2)}) copy-start(f32[64,32]{0,1:T(8,128)} %get-tuple-element.93) | copy-start | bytes 24580
  331.9 9.0 %copy-start.27 = (f32[64,32]{0,1:T(8,128)S(1)}, f32[64,32]{0,1:T(8,128)}, u32[]{:S(2)}) copy-start(f32[64,32]{0,1:T(8,128)} %get-tuple-element.94) | copy-start | bytes 24580
  349.1 9.8 %copy-start.24 = (f32[64,32]{0,1:T(8,128)S(1)}, f32[64,32]{0,1:T(8,128)}, u32[]{:S(2)}) copy-start(f32[64,32]{0,1:T(8,128)} %get-tuple-element.105) | copy-start | bytes 24580
  349.1 9.9 %copy-start.25 = (f32[64,32]{0,1:T(8,128)S(1)}, f32[64,32]{0,1:T(8,128)}, u32[]{:S(2)}) copy-start(f32[64,32]{0,1:T(8,128)} %get-tuple-element.106) | copy-start | bytes 24580
  349.1 27.4 %collective-permute-start = (f32[64,8,129]{2,1,0:T(8,128)}, f32[64,8,129]{2,1,0:T(8,128)}, u32[]{:S(2)}, u32[]{:S(2)}) collective-permute-start(f32[64,8,129]{2,1,0:T(8,128)} %copy.282), channel_id=1, source_target_pairs={{0,2},{2,0},{4,6},{6,4},{8,10},{10,8},{12,14},{14,12},{1,3},{3,1},... | collective-permute-start | bytes 792584 | tf_op jit(solution)/shard_map/ppermute | solution.py:15
  365.0 8.0 %copy-start.53 = (f32[8192]{0:T(1024)S(1)}, f32[8192]{0:T(1024)}, u32[]{:S(2)}) copy-start(f32[8192]{0:T(1024)} %param.19) | copy-start | bytes 98308
  365.0 8.0 %copy-start.55 = (f32[64]{0:T(128)S(1)}, f32[64]{0:T(128)}, u32[]{:S(2)}) copy-start(f32[64]{0:T(128)} %copy-done.54) | copy-start | bytes 772
  370.1 14.9 %collective-permute-start.8 = (f32[64,8,131]{2,1,0:T(8,128)}, f32[64,8,131]{2,1,0:T(8,128)}, u32[]{:S(2)}, u32[]{:S(2)}) collective-permute-start(f32[64,8,131]{2,1,0:T(8,128)} %copy.333), channel_id=1, source_target_pairs={{0,2},{2,0},{4,6},{6,4},{8,10},{10,8},{12,14},{14,12},{1,3},{3,1},... | collective-permute-start | bytes 804872 | tf_op jit(solution)/shard_map/ppermute | solution.py:15
  374.8 8.1 %copy-start.23 = (f32[64,8,2]{0,1,2:T(8,128)S(1)}, f32[64,8,2]{0,1,2:T(8,128)}, u32[]{:S(2)}) copy-start(f32[64,8,2]{0,1,2:T(8,128)} %copy.310) | copy-start | bytes 12292
  411.7 37.3 %collective-permute-start.6 = (f32[64,4096]{1,0:T(8,128)S(1)}, f32[64,4096]{1,0:T(8,128)S(1)}, u32[]{:S(2)}, u32[]{:S(2)}) collective-permute-start(f32[64,4096]{1,0:T(8,128)S(1)} %add.378), channel_id=1, source_target_pairs={{0,4},{2,6},{4,0},{6,2},{8,12},{10,14},{12,8},{14,10},{1,5},{3,7},... | collective-permute-start | bytes 3145736 | tf_op jit(solution)/shard_map/ppermute | solution.py:152
  411.8 10.2 %slice-start = ((s8[8388608]{0:T(1024)(128)(4,1)}), s8[4194304]{0:T(1024)(128)(4,1)S(1)}, s32[]{:S(2)}) async-start(s8[8388608]{0:T(1024)(128)(4,1)} %bitcast.512), calls=%async_computation.6 | async-start | bytes 8388608
  413.6 8.3 %slice-start.1 = ((s8[8388608]{0:T(1024)(128)(4,1)}), s8[4194304]{0:T(1024)(128)(4,1)S(1)}, s32[]{:S(2)}) async-start(s8[8388608]{0:T(1024)(128)(4,1)} %bitcast.512), calls=%async_computation.7 | async-start | bytes 8388608
  413.6 8.3 %copy-start.18 = (bf16[64,512]{1,0:T(8,128)(2,1)S(1)}, bf16[64,512]{1,0:T(8,128)(2,1)}, u32[]{:S(2)}) copy-start(bf16[64,512]{1,0:T(8,128)(2,1)} %reshape.1213) | copy-start | bytes 196612
  413.6 58.2 %collective-permute-start.10 = (f32[64,4096]{1,0:T(8,128)S(1)}, f32[64,4096]{1,0:T(8,128)S(1)}, u32[]{:S(2)}, u32[]{:S(2)}) collective-permute-start(f32[64,4096]{1,0:T(8,128)S(1)} %add.400), channel_id=1, source_target_pairs={{0,4},{2,6},{4,0},{6,2},{8,12},{10,14},{12,8},{14,10},{1,5},{3,7},... | collective-permute-start | bytes 3145736 | tf_op jit(solution)/shard_map/ppermute | solution.py:152
  450.2 84.1 %collective-permute-start.7 = (f32[64,4096]{1,0:T(8,128)}, f32[64,4096]{1,0:T(8,128)}, u32[]{:S(2)}, u32[]{:S(2)}) collective-permute-start(f32[64,4096]{1,0:T(8,128)} %add.379), channel_id=1, source_target_pairs={{0,8},{2,10},{4,12},{6,14},{8,0},{10,2},{12,4},{14,6},{1,9},{3,11}... | collective-permute-start | bytes 3145736 | tf_op jit(solution)/shard_map/ppermute | solution.py:152
  472.9 98.7 %collective-permute-start.11 = (f32[64,4096]{1,0:T(8,128)}, f32[64,4096]{1,0:T(8,128)}, u32[]{:S(2)}, u32[]{:S(2)}) collective-permute-start(f32[64,4096]{1,0:T(8,128)} %add.401), channel_id=1, source_target_pairs={{0,8},{2,10},{4,12},{6,14},{8,0},{10,2},{12,4},{14,6},{1,9},{3,11}... | collective-permute-start | bytes 3145736 | tf_op jit(solution)/shard_map/ppermute | solution.py:152
  587.6 79.0 %all-to-all-start.2 = ((f32[1,64,2,1024]{3,1,0,2:T(8,128)}), f32[1,64,2,1024]{3,1,0,2:T(8,128)}, u32[]{:S(2)}, u32[]{:S(2)}) async-start(f32[1,64,2,1024]{3,1,0,2:T(8,128)} %fusion.57), calls=%async_computation.2 | async-start | bytes 1048576 | tf_op jit(solution)/shard_map/all_to_all | solution.py:161
  662.8 8.1 %copy-start.19 = (f32[8192]{0:T(1024)S(1)}, f32[8192]{0:T(1024)}, u32[]{:S(2)}) copy-start(f32[8192]{0:T(1024)} %param.24) | copy-start | bytes 98308
  666.7 16.0 %all-to-all-start.1 = ((f32[1,64,2,1024]{3,1,0,2:T(8,128)}), f32[1,64,2,1024]{3,1,0,2:T(8,128)}, u32[]{:S(2)}, u32[]{:S(2)}) async-start(f32[1,64,2,1024]{3,1,0,2:T(8,128)} %fusion.54), calls=%async_computation.1 | async-start | bytes 1048576 | tf_op jit(solution)/shard_map/all_to_all | solution.py:161
  682.7 16.9 %all-to-all-start = ((f32[1,64,2,1024]{3,1,0,2:T(8,128)}), f32[1,64,2,1024]{3,1,0,2:T(8,128)}, u32[]{:S(2)}, u32[]{:S(2)}) async-start(f32[1,64,2,1024]{3,1,0,2:T(8,128)} %fusion.51), calls=%async_computation | async-start | bytes 1048576 | tf_op jit(solution)/shard_map/all_to_all | solution.py:161
  699.6 45.4 %copy-start.41 = (s32[64]{0:T(128)S(1)}, s32[64]{0:T(128)}, u32[]{:S(2)}) copy-start(s32[64]{0:T(128)} %get-tuple-element.85) | copy-start | bytes 772
  699.6 45.7 %copy-start.40 = (s32[64]{0:T(128)S(1)}, s32[64]{0:T(128)}, u32[]{:S(2)}) copy-start(s32[64]{0:T(128)} %get-tuple-element.86) | copy-start | bytes 772
  699.6 46.8 %copy-start.39 = (s32[64]{0:T(128)S(1)}, s32[64]{0:T(128)}, u32[]{:S(2)}) copy-start(s32[64]{0:T(128)} %get-tuple-element.84) | copy-start | bytes 772
  (28 other events, 94.3 us)
Sparse Core Ops, SparseCore 0:
  10.8 47.1 all-gather.5
Sparse Core Ops, SparseCore 1:
  138.8 77.3 all-gather.3
  476.0 186.7 all-reduce.4
